TPU v7x, 256 devices: a whole 4x4x8 slice. The times are simulated.
256 devices in a mesh: gx: 2 (over z_hi), gy: 64 (over z_lo, y, x), vert: 2 (over core).
Axes of the slice: x: 4, y: 4, z: 8 (z_hi: 2, z_lo: 4; z = z_hi * 4 + z_lo), core: 2. Of those that a mesh axis runs over, the one named last changes fastest.
Arguments:
- distribution: float32 [32, 1024, 4096], P('gx', 'gy', 'vert'), may hold values from -6 to 6
- density: float32 [32, 1024], P('gx', 'gy'), may hold values from 0.3 to 3
- cell_type: int32 [32, 1024], P('gx', 'gy'), may hold values from 0 to 2, as said below
- inflow: float32 [4096], P('vert'), may hold values from -6 to 6
Outputs:
- evolved: float32 [32, 1024, 4096], P('gx', 'gy', 'vert')
Inputs may be any that keep to these rules, and one draw needn't show every extreme that they name: `cell_type`: 0 marks a gas cell, 1 a wall cell, 2 an inflow cell; most cells are gas cells.
All inputs are finite; a program needn't handle non-finite values.
Results may differ from a plain program's by a relative error of at most 0.0003.
Values sent between devices are 32-bit elements; how exact they have to be, the bound alone decides.
A program may use at most 128 MiB of HBM per device.

v0:
```python
import functools

import jax
import jax.numpy as jnp
from jax import lax
from jax.experimental import pallas as pl
from jax.experimental.pallas import tpu as pltpu
from jax.sharding import PartitionSpec as P

MESH = pl.DeviceIdType.MESH
F32 = jnp.float32
BF16 = jnp.bfloat16

NVX = 64
HALF = 32
STEPS = 2
SPACING = 8.0 / NVX
TIME_STEP = 0.1
COLLISION_RATE = 0.2
GAIN_SCALE = 2.0 * 2.5 * SPACING * SPACING / 4.0
LOG2E = 1.4426950408889634

ROWS = 16
COLS = 16
LOCAL = 2048
PAD_X = ROWS + 4
PAD_Y = 32
TOP = 8


def iota(shape, dim):
    return lax.broadcasted_iota(jnp.int32, shape, dim)


def as_f32(x):
    return x.astype(F32)


def clamp_slope(a, b):
    return jnp.minimum(jnp.maximum(b, jnp.minimum(a, 0.0)), jnp.maximum(a, 0.0))


def split(x):
    hi = x.astype(BF16)
    lo = (x - hi.astype(F32)).astype(BF16)
    return hi, lo


def mm(a, b):
    return jnp.dot(a, b, preferred_element_type=F32)


def parity_maps(h_ref):
    row, col = iota((256, 256), 0), iota((256, 256), 1)
    for k in range(4):
        lane, out = (row, col) if k < 2 else (col, row)
        odd, out_i, b = out // 128, (out // 32) % 4, out % 32
        lane_i, j = lane // 64, lane % 64
        same = lane_i == (out_i if k % 2 == 0 else 3 - out_i)
        upper = (j == HALF + b) & same
        lower = (j == HALF - 1 - b) & same
        value = jnp.where(upper, 1.0, jnp.where(lower, jnp.where(odd == 1, -1.0, 1.0), 0.0))
        h_ref[k] = value.astype(BF16)


def magnitude(i, vt):
    return (jnp.where(vt == 1, as_f32(i), (HALF - 1.0) - as_f32(i)) + 0.5) * SPACING


def make_kernel_blocks(vt, khi, klo):
    qv = (as_f32(iota((32, 128), 1) % 32) + 0.5) * SPACING
    qw = (as_f32(iota((32, 128), 0)) + 0.5) * SPACING
    dy = ((qv - qw) * (qv - qw) + SPACING * SPACING, (qv + qw) * (qv + qw) + SPACING * SPACING)
    ey = qv * qv - qw * qw
    gy = jnp.exp(-(qv * qv + qw * qw) / 4.0) * 0.5
    lane_i = iota((1, 128), 1) // 32

    def tile(t, carry):
        n, i = t // 32, t % 32
        pv = magnitude(n * 4 + lane_i, vt)
        pw = magnitude(jnp.zeros((1, 128), jnp.int32) + i, vt)
        e = ey + (pv * pv - pw * pw)
        e2 = e * e
        g = gy * jnp.exp(-(pv * pv + pw * pw) / 4.0)
        dx = ((pv - pw) * (pv - pw), (pv + pw) * (pv + pw))
        parts = []
        for a in range(2):
            for b in range(2):
                r2 = dy[b] + dx[a]
                rs = lax.rsqrt(r2)
                arg = (r2 + e2 * (rs * rs)) * (-LOG2E / 8.0)
                parts.append(jnp.exp2(arg) * rs - (r2 * rs) * g)
        mm_, mp, pm, pp = parts
        sm, dm = mm_ + mp, mm_ - mp
        sp, dp = pm + pp, pm - pp
        blocks = (sm + sp, dm + dp, sm - sp, dm - dp)
        at = pl.ds(pl.multiple_of(i * 32, 32), 32)
        lanes = pl.ds(pl.multiple_of(n * 128, 128), 128)
        for k in range(4):
            hi, lo = split(blocks[k])
            khi[k, at, lanes] = hi
            klo[k, at, lanes] = lo
        return carry

    lax.fori_loop(0, 256, tile, 0)


def advect(vt, pad, adv):
    lane = iota((1, 128), 1)
    vy = (as_f32(lane % 64) - 0.5 * (NVX - 1)) * SPACING
    ay = TIME_STEP * jnp.abs(vy)
    cy = 0.5 * ay * (1.0 - ay)
    forward = jnp.broadcast_to(vy > 0, (COLS, 128))
    sign = 2 * vt - 1
    first = 2 + (1 - vt) * (ROWS - 1)

    def chunk(m, carry):
        lanes = pl.ds(pl.multiple_of(m * 128, 128), 128)
        index = vt * HALF + m * 2 + lane // 64
        ax = TIME_STEP * jnp.abs((as_f32(index) - 0.5 * (NVX - 1)) * SPACING)
        cx = 0.5 * ax * (1.0 - ax)

        def row(px):
            return pad[px, TOP:TOP + COLS, lanes]

        u2, u1 = row(first - 2 * sign), row(first - sign)
        here = row(first)
        d0 = here - u1
        s1 = clamp_slope(u1 - u2, d0)
        for k in range(ROWS):
            px = first + k * sign
            ahead = row(px + sign)
            dw = ahead - here
            s0 = clamp_slope(d0, dw)
            term_x = ax * d0 + cx * (s0 - s1)
            l1 = pad[px, TOP - 1:TOP - 1 + COLS, lanes]
            l2 = pad[px, TOP - 2:TOP - 2 + COLS, lanes]
            r1 = pad[px, TOP + 1:TOP + 1 + COLS, lanes]
            r2 = pad[px, TOP + 2:TOP + 2 + COLS, lanes]
            v1 = jnp.where(forward, l1, r1)
            v2 = jnp.where(forward, l2, r2)
            w1 = jnp.where(forward, r1, l1)
            e0 = here - v1
            t0 = clamp_slope(e0, w1 - here)
            t1 = clamp_slope(v1 - v2, e0)
            term_y = ay * e0 + cy * (t0 - t1)
            out = here - term_x - term_y
            x = px - 2
            adv[0, x, :, lanes] = out[:8]
            adv[1, x, :, lanes] = out[8:]
            here, d0, s1 = ahead, dw, s0
        return carry

    lax.fori_loop(0, LOCAL // 128, chunk, 0)


def flat(ref):
    return ref.reshape(128, LOCAL)


def to_parities(own, other, h_ref, s_ref):
    own, other = flat(own), flat(other)

    def chunk(n, carry):
        hi, lo = split(own[:, pl.ds(pl.multiple_of(n * 256, 256), 256)])
        y = mm(hi, h_ref[0]) + mm(lo, h_ref[0])
        hi, lo = split(other[:, pl.ds(pl.multiple_of((7 - n) * 256, 256), 256)])
        z = mm(hi, h_ref[1]) + mm(lo, h_ref[1])
        lanes = pl.ds(pl.multiple_of(n * 128, 128), 128)
        for k, value in enumerate((y + z, y - z)):
            hi, lo = split(value)
            for odd in range(2):
                s_ref[2 * k + odd, :128, lanes] = hi[:, 128 * odd:128 * odd + 128]
                s_ref[2 * k + odd, 128:, lanes] = lo[:, 128 * odd:128 * odd + 128]
        return carry

    lax.fori_loop(0, 8, chunk, 0)


def contract(s_ref, khi, klo, g_ref):
    def tile(t, carry):
        k, n = t // 4, t % 4
        lanes = pl.ds(pl.multiple_of(n * 256, 256), 256)
        both = mm(s_ref[k], khi[k, :, lanes])
        rest = mm(s_ref[k, :128, :], klo[k, :, lanes])
        g_ref[k, :, lanes] = both[:128] + both[128:] + rest
        return carry

    lax.fori_loop(0, 16, tile, 0)


def from_parities(g_ref, h_ref, own, other):
    own, other = flat(own), flat(other)

    def chunk(n, carry):
        lanes = pl.ds(pl.multiple_of(n * 128, 128), 128)
        even = jnp.concatenate([g_ref[0, :, lanes], g_ref[1, :, lanes]], axis=1)
        odd = jnp.concatenate([g_ref[2, :, lanes], g_ref[3, :, lanes]], axis=1)
        hi, lo = split(even + odd)
        own[:, pl.ds(pl.multiple_of(n * 256, 256), 256)] = mm(hi, h_ref[2]) + mm(lo, h_ref[2])
        hi, lo = split(even - odd)
        other[:, pl.ds(pl.multiple_of((7 - n) * 256, 256), 256)] = mm(hi, h_ref[3]) + mm(lo, h_ref[3])
        return carry

    lax.fori_loop(0, 8, chunk, 0)


def collide(vt, adv, gains, dens_b, type_b, inflow, put):
    lane = iota((1, 128), 1)
    vy = (as_f32(lane % 64) - 0.5 * (NVX - 1)) * SPACING

    def chunk(m, carry):
        lanes = pl.ds(pl.multiple_of(m * 128, 128), 128)
        index = vt * HALF + m * 2 + lane // 64
        vx = (as_f32(index) - 0.5 * (NVX - 1)) * SPACING
        nu = 1.0 + (vx * vx + vy * vy) / 8.0
        held = inflow[:, lanes]
        for x in range(ROWS):
            for half in range(2):
                a = adv[half, x, :, lanes]
                gain = gains[half, x, :, lanes] * GAIN_SCALE
                rate = dens_b[x, 8 * half:8 * half + 8, :]
                kind = type_b[x, 8 * half:8 * half + 8, :]
                after = a + rate * (gain - nu * a)
                after = jnp.where(kind == 1, 0.0, jnp.where(kind == 2, held, after))
                put(x, half, lanes, after)
        return carry

    lax.fori_loop(0, LOCAL // 128, chunk, 0)


def kernel(dist, density, cell_type, inflow, out, pads, packs, halos, adv, fin, gains, gsend, s_ref, g_ref,
           khi, klo, h_ref, dens_b, type_b, load_sem, xsend, xrecv, ysend, yrecv, fsend, frecv, qsend, qrecv):
    gx, gy, vt = lax.axis_index("gx"), lax.axis_index("gy"), lax.axis_index("vert")
    last = lax.axis_size("gy") - 1
    has_left, has_right = gy > 0, gy < last
    gets_two = gx == vt

    load = pltpu.make_async_copy(dist, pads.at[0, pl.ds(2, ROWS), pl.ds(TOP, COLS), :], load_sem)
    load.start()

    barrier = pltpu.get_barrier_semaphore()
    pl.semaphore_signal(barrier, inc=1, device_id=(1 - gx, gy, vt), device_id_type=MESH)
    pl.semaphore_signal(barrier, inc=1, device_id=(gx, gy, 1 - vt), device_id_type=MESH)

    @pl.when(has_left)
    def _():
        pl.semaphore_signal(barrier, inc=1, device_id=(gx, gy - 1, vt), device_id_type=MESH)

    @pl.when(has_right)
    def _():
        pl.semaphore_signal(barrier, inc=1, device_id=(gx, gy + 1, vt), device_id_type=MESH)

    pl.semaphore_wait(barrier, 2 + has_left.astype(jnp.int32) + has_right.astype(jnp.int32))

    def x_copy(step, count):
        if count == 2:
            start, to = (1 - gx) * (ROWS - 2), gx * (ROWS + 2)
        else:
            start, to = (1 - gx) * (ROWS - 1), 1 + gx * (ROWS + 1)
        return pltpu.make_async_remote_copy(
            src_ref=pads.at[step, pl.ds(2 + start, count), pl.ds(TOP, COLS), :],
            dst_ref=pads.at[step, pl.ds(to, count), pl.ds(TOP, COLS), :],
            send_sem=xsend.at[step], recv_sem=xrecv.at[step],
            device_id=(1 - gx, gy, vt), device_id_type=MESH)

    def y_copy(step, side):
        return pltpu.make_async_remote_copy(
            src_ref=packs.at[step, side], dst_ref=halos.at[step, 1 - side],
            send_sem=ysend.at[step, side], recv_sem=yrecv.at[step, 1 - side],
            device_id=(gx, gy - 1 + 2 * side, vt), device_id_type=MESH)

    def y_wait(step, side):
        return pltpu.make_async_remote_copy(
            src_ref=packs.at[step, side], dst_ref=halos.at[step, side],
            send_sem=ysend.at[step, side], recv_sem=yrecv.at[step, side],
            device_id=(gx, gy - 1 + 2 * side, vt), device_id_type=MESH)

    def x_wait(step, count):
        if count == 2:
            to = (1 - gx) * (ROWS + 2)
        else:
            to = 1 + (1 - gx) * (ROWS + 1)
        return pltpu.make_async_remote_copy(
            src_ref=pads.at[step, pl.ds(to, count), pl.ds(TOP, COLS), :],
            dst_ref=pads.at[step, pl.ds(to, count), pl.ds(TOP, COLS), :],
            send_sem=xsend.at[step], recv_sem=xrecv.at[step],
            device_id=(1 - gx, gy, vt), device_id_type=MESH)

    def send_halos(step):
        @pl.when(gets_two)
        def _():
            x_copy(step, 1).start()

        @pl.when(jnp.logical_not(gets_two))
        def _():
            x_copy(step, 2).start()

        for side, present in ((0, has_left), (1, has_right)):
            y = TOP + side * (COLS - 2)
            for x in range(ROWS):
                at = 2 * (x % 4)
                packs[step, side, x // 4, at:at + 2, :] = pads[step, 2 + x, y:y + 2, :]
            pl.when(present)(lambda side=side: y_copy(step, side).start())

    def clear_missing(step):
        zero_row = jnp.zeros((COLS, LOCAL), F32)

        @pl.when(gets_two)
        def _():
            pads[step, 1 + (1 - vt) * 0 + vt * (ROWS + 1), pl.ds(TOP, COLS), :] = zero_row

        @pl.when(jnp.logical_not(gets_two))
        def _():
            for k in range(2):
                pads[step, (1 - vt) * (ROWS + 2) + k, pl.ds(TOP, COLS), :] = zero_row

        for side, present in ((0, has_left), (1, has_right)):
            @pl.when(jnp.logical_not(present))
            def _():
                for group in range(4):
                    halos[step, side, group] = jnp.zeros((8, LOCAL), F32)

    def take_halos(step):
        @pl.when(gets_two)
        def _():
            x_wait(step, 2).wait_recv()

        @pl.when(jnp.logical_not(gets_two))
        def _():
            x_wait(step, 1).wait_recv()

        for side, present in ((0, has_left), (1, has_right)):
            pl.when(present)(lambda side=side: y_wait(step, side).wait_recv())
            y = TOP - 2 + side * (COLS + 2)
            for x in range(ROWS):
                at = 2 * (x % 4)
                pads[step, 2 + x, y:y + 2, :] = halos[step, side, x // 4, at:at + 2, :]

    def wait_sent(step):
        @pl.when(gets_two)
        def _():
            x_copy(step, 1).wait_send()

        @pl.when(jnp.logical_not(gets_two))
        def _():
            x_copy(step, 2).wait_send()

        for side, present in ((0, has_left), (1, has_right)):
            pl.when(present)(lambda side=side: y_copy(step, side).wait_send())

    def partner_copy(src, dst, step, send, recv):
        return pltpu.make_async_remote_copy(
            src_ref=src, dst_ref=dst, send_sem=send.at[step], recv_sem=recv.at[step],
            device_id=(gx, gy, 1 - vt), device_id_type=MESH)

    load.wait()
    send_halos(0)
    for step in range(STEPS):
        clear_missing(step)
    rate = (COLLISION_RATE * density[...]).T
    kind = as_f32(cell_type[...]).T
    for x in range(ROWS):
        dens_b[x] = jnp.broadcast_to(rate[:, x:x + 1], (COLS, 128))
        type_b[x] = jnp.broadcast_to(kind[:, x:x + 1], (COLS, 128))
    parity_maps(h_ref)
    make_kernel_blocks(vt, khi, klo)

    for step in range(STEPS):
        take_halos(step)
        advect(vt, pads.at[step], adv)
        there = partner_copy(adv.at[1 - vt], fin.at[step], step, fsend, frecv)
        there.start()
        there.wait()
        to_parities(adv.at[vt], fin.at[step], h_ref, s_ref)
        contract(s_ref, khi, klo, g_ref)
        from_parities(g_ref, h_ref, gains.at[step, vt], gsend.at[step])
        back = partner_copy(gsend.at[step], gains.at[step, vt], step, qsend, qrecv)
        back.start()
        partner_copy(gsend.at[step], gains.at[step, 1 - vt], step, qsend, qrecv).wait_recv()
        back.wait_send()
        if step < STEPS - 1:
            def put(x, half, lanes, value):
                pads[step + 1, 2 + x, TOP + 8 * half:TOP + 8 * half + 8, lanes] = value
        else:
            def put(x, half, lanes, value):
                out[x, 8 * half:8 * half + 8, lanes] = value
        collide(vt, adv, gains.at[step], dens_b, type_b, inflow, put)
        wait_sent(step)
        if step < STEPS - 1:
            send_halos(step + 1)


def per_device(distribution, density, cell_type, inflow):
    vmem = pl.BlockSpec(memory_space=pltpu.VMEM)
    dma = pltpu.SemaphoreType.DMA
    return pl.pallas_call(
        kernel,
        out_shape=jax.ShapeDtypeStruct((ROWS, COLS, LOCAL), F32),
        in_specs=[pl.BlockSpec(memory_space=pl.ANY), vmem, vmem, vmem],
        out_specs=vmem,
        scratch_shapes=[
            pltpu.VMEM((STEPS, PAD_X, PAD_Y, LOCAL), F32),
            pltpu.VMEM((STEPS, 2, 4, 8, LOCAL), F32),
            pltpu.VMEM((STEPS, 2, 4, 8, LOCAL), F32),
            pltpu.VMEM((2, ROWS, 8, LOCAL), F32),
            pltpu.VMEM((STEPS, ROWS, 8, LOCAL), F32),
            pltpu.VMEM((STEPS, 2, ROWS, 8, LOCAL), F32),
            pltpu.VMEM((STEPS, ROWS, 8, LOCAL), F32),
            pltpu.VMEM((4, 256, 1024), BF16),
            pltpu.VMEM((4, 128, 1024), F32),
            pltpu.VMEM((4, 1024, 1024), BF16),
            pltpu.VMEM((4, 1024, 1024), BF16),
            pltpu.VMEM((4, 256, 256), BF16),
            pltpu.VMEM((ROWS, COLS, 128), F32),
            pltpu.VMEM((ROWS, COLS, 128), F32),
            dma,
            dma((STEPS,)), dma((STEPS,)),
            dma((STEPS, 2)), dma((STEPS, 2)),
            dma((STEPS,)), dma((STEPS,)),
            dma((STEPS,)), dma((STEPS,)),
        ],
        compiler_params=pltpu.CompilerParams(
            collective_id=0, has_side_effects=True, vmem_limit_bytes=67000000),
    )(distribution, density, cell_type, inflow.reshape(1, LOCAL))


def solution(mesh):
    placed = (P("gx", "gy", "vert"), P("gx", "gy"), P("gx", "gy"), P("vert"))
    return jax.shard_map(
        per_device, mesh=mesh, in_specs=placed, out_specs=P("gx", "gy", "vert"), check_vma=False
    )
```

profile of v0, /device:TPU:33, one launch (start us, length us, event | category | flops | bytes accessed | tf_op | source)
XLA Modules:
  0.0 91.2 jit_solution(14346228250644216850)
XLA Ops:
  0.0 88.0 %shard_map.46 = f32[16,16,2048]{2,1,0:T(8,128)} custom-call(f32[16,16,2048]{2,1,0:T(8,128)} %dist.1, f32[16,16]{1,0:T(8,128)} %density.1, s32[16,16]{1,0:T(8,128)} %cell_type.1, f32[1,2048]{1,0:T(1,128)} %bitcast.1), custom_call_target="tpu_custom_call" | custom-call | tf_op jit(solution)/shard_map/pallas_call | solution.py:397
  88.0 3.1 %copy.6 = f32[16,16,2048]{2,1,0:T(8,128)} copy(f32[16,16,2048]{2,1,0:T(8,128)} %shard_map.46) | data formatting | bytes 4194304
where the time goes:
time: 91.3 us; the launch traced here: 91.2 us
  Pallas kernels  88 us (96%)
  local copies, waits for them, and re-layouts  3.14 us (3%)
    pallas_call x1, Pallas kernels, per_device(): pl.pallas_call(kernel, out_shape=jax.ShapeDtypeStruct((ROWS, COLS, LOCAL)...  88 us
    unnamed x1, local copies, waits for them, and re-layouts  3.14 us

commit v1 on v0

v1 whole, which is shorter than its diff:
```python
import functools

import jax
import jax.numpy as jnp
from jax import lax
from jax.experimental import pallas as pl
from jax.experimental.pallas import tpu as pltpu
from jax.sharding import PartitionSpec as P

MESH = pl.DeviceIdType.MESH
F32 = jnp.float32
BF16 = jnp.bfloat16

NVX = 64
HALF = 32
STEPS = 2
SPACING = 8.0 / NVX
TIME_STEP = 0.1
COLLISION_RATE = 0.2
GAIN_SCALE = 2.0 * 2.5 * SPACING * SPACING / 4.0
LOG2E = 1.4426950408889634

ROWS = 16
COLS = 16
GROUP = 8
CELLS = GROUP * COLS
LOCAL = 2048
PAD_X = ROWS + 4
PAD_Y = 32
TOP = 8


def iota(shape, dim):
    return lax.broadcasted_iota(jnp.int32, shape, dim)


def as_f32(x):
    return x.astype(F32)


def clamp_slope(a, b):
    return jnp.minimum(jnp.maximum(b, jnp.minimum(a, 0.0)), jnp.maximum(a, 0.0))


def split(x):
    hi = x.astype(BF16)
    lo = (x - hi.astype(F32)).astype(BF16)
    return hi, lo


def mm(a, b):
    return jnp.dot(a, b, preferred_element_type=F32)


def parity_maps(vt, h_ref):
    row, col = iota((256, 256), 0), iota((256, 256), 1)
    for k, (lane, out) in enumerate(((row, col), (col, row))):
        odd, out_i, b = out // 128, (out // 32) % 4, out % 32
        lane_i, j = lane // 64, lane % 64
        same = lane_i == jnp.where(vt == 1, out_i, 3 - out_i)
        upper = (j == HALF + b) & same
        lower = (j == HALF - 1 - b) & same
        value = jnp.where(upper, 1.0, jnp.where(lower, jnp.where(odd == 1, -1.0, 1.0), 0.0))
        h_ref[k] = value.astype(BF16)


def magnitude(i):
    return (as_f32(i) + 0.5) * SPACING


def make_kernel_blocks(vt, khi, klo):
    qv = (as_f32(iota((32, 128), 1) % 32) + 0.5) * SPACING
    qw = (as_f32(iota((32, 128), 0)) + 0.5) * SPACING
    dy = ((qv - qw) * (qv - qw) + SPACING * SPACING, (qv + qw) * (qv + qw) + SPACING * SPACING)
    ey = qv * qv - qw * qw
    gy = jnp.exp(-(qv * qv + qw * qw) / 4.0) * 0.5
    lane_i = iota((1, 128), 1) // 32
    sign = as_f32(1 - 2 * vt)

    def tile(t, carry):
        n, i = t // 32, t % 32
        pv = magnitude(n * 4 + lane_i)
        pw = magnitude(jnp.zeros((1, 128), jnp.int32) + i)
        e = ey + (pv * pv - pw * pw)
        e2 = e * e
        g = gy * jnp.exp(-(pv * pv + pw * pw) / 4.0)
        dx = ((pv - pw) * (pv - pw), (pv + pw) * (pv + pw))
        parts = []
        for a in range(2):
            for b in range(2):
                r2 = dy[b] + dx[a]
                rs = lax.rsqrt(r2)
                arg = (r2 + e2 * (rs * rs)) * (-LOG2E / 8.0)
                parts.append(jnp.exp2(arg) * rs - (r2 * rs) * g)
        mm_, mp, pm, pp = parts
        sm, dm = mm_ + mp, mm_ - mp
        sp, dp = pm + pp, pm - pp
        blocks = (sm + sign * sp, dm + sign * dp)
        at = pl.ds(pl.multiple_of(i * 32, 32), 32)
        lanes = pl.ds(pl.multiple_of(n * 128, 128), 128)
        for k in range(2):
            hi, lo = split(blocks[k])
            khi[k, at, lanes] = hi
            klo[k, at, lanes] = lo
        return carry

    lax.fori_loop(0, 256, tile, 0)


def advect(vt, pad, base, adv):
    lane = iota((1, 128), 1)
    vy = (as_f32(lane % 64) - 0.5 * (NVX - 1)) * SPACING
    ay = TIME_STEP * jnp.abs(vy)
    cy = 0.5 * ay * (1.0 - ay)
    forward = jnp.broadcast_to(vy > 0, (COLS, 128))
    sign = 2 * vt - 1
    offset = (1 - vt) * (GROUP - 1)
    first = 2 + base + offset

    def chunk(m, carry):
        lanes = pl.ds(pl.multiple_of(m * 128, 128), 128)
        index = vt * HALF + m * 2 + lane // 64
        ax = TIME_STEP * jnp.abs((as_f32(index) - 0.5 * (NVX - 1)) * SPACING)
        cx = 0.5 * ax * (1.0 - ax)

        def row(px):
            return pad[px, TOP:TOP + COLS, lanes]

        u2, u1 = row(first - 2 * sign), row(first - sign)
        here = row(first)
        d0 = here - u1
        s1 = clamp_slope(u1 - u2, d0)
        for k in range(GROUP):
            px = first + k * sign
            ahead = row(px + sign)
            dw = ahead - here
            s0 = clamp_slope(d0, dw)
            term_x = ax * d0 + cx * (s0 - s1)
            l1 = pad[px, TOP - 1:TOP - 1 + COLS, lanes]
            l2 = pad[px, TOP - 2:TOP - 2 + COLS, lanes]
            r1 = pad[px, TOP + 1:TOP + 1 + COLS, lanes]
            r2 = pad[px, TOP + 2:TOP + 2 + COLS, lanes]
            v1 = jnp.where(forward, l1, r1)
            v2 = jnp.where(forward, l2, r2)
            w1 = jnp.where(forward, r1, l1)
            e0 = here - v1
            t0 = clamp_slope(e0, w1 - here)
            t1 = clamp_slope(v1 - v2, e0)
            term_y = ay * e0 + cy * (t0 - t1)
            adv[offset + k * sign, :, lanes] = here - term_x - term_y
            here, d0, s1 = ahead, dw, s0
        return carry

    lax.fori_loop(0, LOCAL // 128, chunk, 0)


def wide(n):
    return pl.ds(pl.multiple_of(n * 256, 256), 256)


def stack(n, value, t_ref):
    hi, lo = split(value)
    t_ref[128 * n:128 * n + 128, :] = hi
    t_ref[1024 + 128 * n:1024 + 128 * n + 128, :] = lo


def to_parities(vt, adv, h_ref, t_ref, y_ref):
    cells = adv.reshape(CELLS, LOCAL)
    for n in range(8):
        stack(n, cells[:, wide(jnp.where(vt == 1, n, 7 - n))], t_ref)
    y = mm(t_ref[...], h_ref[0])
    for n in range(8):
        value = y[128 * n:128 * n + 128] + y[1024 + 128 * n:1024 + 128 * n + 128]
        for odd in range(2):
            y_ref[odd, :, 128 * n:128 * n + 128] = value[:, 128 * odd:128 * odd + 128]


def contract(vt, own, other, khi, klo, g_ref):
    sign = as_f32(1 - 2 * vt)
    for k in range(2):
        hi, lo = split(own[k] + sign * other[k])
        both = mm(jnp.concatenate([hi, lo], axis=0), khi[k])
        g_ref[k] = both[:CELLS] + both[CELLS:] + mm(hi, klo[k])


def from_parities(vt, own, other, h_ref, t_ref, adv, dens, kinds, inflow, put):
    sign = as_f32(2 * vt - 1)
    cells = adv.reshape(CELLS, LOCAL)
    for n in range(8):
        at = slice(128 * n, 128 * n + 128)
        stack(n, jnp.concatenate([own[k, :, at] + sign * other[k, :, at] for k in range(2)], axis=1), t_ref)
    back = mm(t_ref[...], h_ref[1])
    lane = iota((1, 256), 1)
    vy = (as_f32(lane % 64) - 0.5 * (NVX - 1)) * SPACING
    rate, kind = (jnp.concatenate([ref[...]] * 2, axis=1) for ref in (dens, kinds))
    for n in range(8):
        m = jnp.where(vt == 1, n, 7 - n)
        gain = (back[128 * n:128 * n + 128] + back[1024 + 128 * n:1024 + 128 * n + 128]) * GAIN_SCALE
        vx = (as_f32(vt * HALF + m * 4 + lane // 64) - 0.5 * (NVX - 1)) * SPACING
        nu = 1.0 + (vx * vx + vy * vy) / 8.0
        a = cells[:, wide(m)]
        after = a + rate * (gain - nu * a)
        after = jnp.where(kind == 1, 0.0, jnp.where(kind == 2, inflow[:, wide(m)], after))
        put(wide(m), after.reshape(GROUP, COLS, 256))


def kernel(dist, density, cell_type, inflow, out, pads, packs, halos, adv, yown, yin, gown, gin, t_ref,
           khi, klo, h_ref, dens_b, type_b, load_sem, xsend, xrecv, ysend, yrecv, fsend, frecv, qsend, qrecv):
    gx, gy, vt = lax.axis_index("gx"), lax.axis_index("gy"), lax.axis_index("vert")
    last = lax.axis_size("gy") - 1
    has_left, has_right = gy > 0, gy < last
    gets_two = gx == vt
    sides = ((0, has_left), (1, has_right))
    bases = ((1 - gx) * GROUP, gx * GROUP)

    load = pltpu.make_async_copy(dist, pads.at[0, pl.ds(2, ROWS), pl.ds(TOP, COLS), :], load_sem)
    load.start()

    barrier = pltpu.get_barrier_semaphore()
    pl.semaphore_signal(barrier, inc=1, device_id=(1 - gx, gy, vt), device_id_type=MESH)
    pl.semaphore_signal(barrier, inc=1, device_id=(gx, gy, 1 - vt), device_id_type=MESH)

    @pl.when(has_left)
    def _():
        pl.semaphore_signal(barrier, inc=1, device_id=(gx, gy - 1, vt), device_id_type=MESH)

    @pl.when(has_right)
    def _():
        pl.semaphore_signal(barrier, inc=1, device_id=(gx, gy + 1, vt), device_id_type=MESH)

    def x_copy(step, count):
        if count == 2:
            start, to = (1 - gx) * (ROWS - 2), gx * (ROWS + 2)
        else:
            start, to = (1 - gx) * (ROWS - 1), 1 + gx * (ROWS + 1)
        return pltpu.make_async_remote_copy(
            src_ref=pads.at[step, pl.ds(2 + start, count), pl.ds(TOP, COLS), :],
            dst_ref=pads.at[step, pl.ds(to, count), pl.ds(TOP, COLS), :],
            send_sem=xsend.at[step], recv_sem=xrecv.at[step],
            device_id=(1 - gx, gy, vt), device_id_type=MESH)

    def x_wait(step, count):
        if count == 2:
            to = (1 - gx) * (ROWS + 2)
        else:
            to = 1 + (1 - gx) * (ROWS + 1)
        return pltpu.make_async_remote_copy(
            src_ref=pads.at[step, pl.ds(to, count), pl.ds(TOP, COLS), :],
            dst_ref=pads.at[step, pl.ds(to, count), pl.ds(TOP, COLS), :],
            send_sem=xsend.at[step], recv_sem=xrecv.at[step],
            device_id=(1 - gx, gy, vt), device_id_type=MESH)

    def y_copy(step, group, side, to):
        return pltpu.make_async_remote_copy(
            src_ref=packs.at[step, group, side], dst_ref=halos.at[step, group, to],
            send_sem=ysend.at[step, group, side], recv_sem=yrecv.at[step, group, to],
            device_id=(gx, gy - 1 + 2 * side, vt), device_id_type=MESH)

    def send_x(step):
        pl.when(gets_two)(lambda: x_copy(step, 1).start())
        pl.when(jnp.logical_not(gets_two))(lambda: x_copy(step, 2).start())

    def send_y(step, group):
        for side, present in sides:
            y = TOP + side * (COLS - 2)
            for x in range(GROUP):
                at = 2 * (x % 4)
                packs[step, group, side, x // 4, at:at + 2, :] = pads[step, 2 + bases[group] + x, y:y + 2, :]
            pl.when(present)(lambda side=side: y_copy(step, group, side, 1 - side).start())

    def clear_missing(step):
        zero_row = jnp.zeros((COLS, LOCAL), F32)

        @pl.when(gets_two)
        def _():
            pads[step, 1 + vt * (ROWS + 1), pl.ds(TOP, COLS), :] = zero_row

        @pl.when(jnp.logical_not(gets_two))
        def _():
            for k in range(2):
                pads[step, (1 - vt) * (ROWS + 2) + k, pl.ds(TOP, COLS), :] = zero_row

        for side, present in sides:
            @pl.when(jnp.logical_not(present))
            def _():
                for group in range(2):
                    for part in range(2):
                        halos[step, group, side, part] = jnp.zeros((8, LOCAL), F32)

    def take_x(step):
        pl.when(gets_two)(lambda: x_wait(step, 2).wait_recv())
        pl.when(jnp.logical_not(gets_two))(lambda: x_wait(step, 1).wait_recv())

    def take_y(step, group):
        for side, present in sides:
            pl.when(present)(lambda side=side: y_copy(step, group, side, side).wait_recv())
            y = TOP - 2 + side * (COLS + 2)
            for x in range(GROUP):
                at = 2 * (x % 4)
                pads[step, 2 + bases[group] + x, y:y + 2, :] = halos[step, group, side, x // 4, at:at + 2, :]

    def wait_sent(step):
        pl.when(gets_two)(lambda: x_copy(step, 1).wait_send())
        pl.when(jnp.logical_not(gets_two))(lambda: x_copy(step, 2).wait_send())
        for group in range(2):
            for side, present in sides:
                pl.when(present)(lambda side=side, group=group: y_copy(step, group, side, side).wait_send())

    def partner_copy(src, dst, send, recv, step, group):
        return pltpu.make_async_remote_copy(
            src_ref=src.at[step, group], dst_ref=dst.at[step, group],
            send_sem=send.at[step, group], recv_sem=recv.at[step, group],
            device_id=(gx, gy, 1 - vt), device_id_type=MESH)

    def there(step, group):
        return partner_copy(yown, yin, fsend, frecv, step, group)

    def back(step, group):
        return partner_copy(gown, gin, qsend, qrecv, step, group)

    def stage_a(step, group):
        advect(vt, pads.at[step], bases[group], adv.at[group])

    def stage_t(step, group):
        to_parities(vt, adv.at[group], h_ref, t_ref, yown.at[step, group])
        there(step, group).start()

    def stage_c(step, group):
        there(step, group).wait_recv()
        contract(vt, yown.at[step, group], yin.at[step, group], khi, klo, gown.at[step, group])
        back(step, group).start()

    def stage_f(step, group):
        back(step, group).wait_recv()
        base = bases[group]
        if step < STEPS - 1:
            def put(lanes, value):
                pads[step + 1, pl.ds(2 + base, GROUP), TOP:TOP + COLS, lanes] = value
        else:
            def put(lanes, value):
                out[pl.ds(base, GROUP), :, lanes] = value
        cells = pl.ds(pl.multiple_of(base * COLS, CELLS), CELLS)
        from_parities(vt, gown.at[step, group], gin.at[step, group], h_ref, t_ref, adv.at[group],
                      dens_b.at[cells], type_b.at[cells], inflow, put)

    load.wait()
    pl.semaphore_wait(barrier, 2 + has_left.astype(jnp.int32) + has_right.astype(jnp.int32))
    send_x(0)
    for group in range(2):
        send_y(0, group)
    for step in range(STEPS):
        clear_missing(step)
    rate = (COLLISION_RATE * density[...]).T
    kind = as_f32(cell_type[...]).T
    for x in range(ROWS):
        dens_b[x * COLS:x * COLS + COLS] = jnp.broadcast_to(rate[:, x:x + 1], (COLS, 128))
        type_b[x * COLS:x * COLS + COLS] = jnp.broadcast_to(kind[:, x:x + 1], (COLS, 128))
    parity_maps(vt, h_ref)
    make_kernel_blocks(vt, khi, klo)

    take_y(0, 1)
    stage_a(0, 1)
    take_y(0, 0)
    take_x(0)
    stage_a(0, 0)
    stage_t(0, 0)
    stage_t(0, 1)
    stage_c(0, 0)
    stage_c(0, 1)
    stage_f(0, 0)
    send_x(1)
    send_y(1, 0)
    stage_f(0, 1)
    send_y(1, 1)
    take_y(1, 1)
    stage_a(1, 1)
    stage_t(1, 1)
    stage_c(1, 1)
    take_y(1, 0)
    take_x(1)
    stage_a(1, 0)
    stage_t(1, 0)
    stage_f(1, 1)
    stage_c(1, 0)
    stage_f(1, 0)
    for step in range(STEPS):
        wait_sent(step)
        for group in range(2):
            there(step, group).wait_send()
            back(step, group).wait_send()


def per_device(distribution, density, cell_type, inflow):
    vmem = pl.BlockSpec(memory_space=pltpu.VMEM)
    dma = pltpu.SemaphoreType.DMA
    pair = pltpu.VMEM((STEPS, 2, 2, CELLS, 1024), F32)
    return pl.pallas_call(
        kernel,
        out_shape=jax.ShapeDtypeStruct((ROWS, COLS, LOCAL), F32),
        in_specs=[pl.BlockSpec(memory_space=pl.ANY), vmem, vmem, vmem],
        out_specs=vmem,
        scratch_shapes=[
            pltpu.VMEM((STEPS, PAD_X, PAD_Y, LOCAL), F32),
            pltpu.VMEM((STEPS, 2, 2, 2, 8, LOCAL), F32),
            pltpu.VMEM((STEPS, 2, 2, 2, 8, LOCAL), F32),
            pltpu.VMEM((2, GROUP, COLS, LOCAL), F32),
            pair, pair, pair, pair,
            pltpu.VMEM((2048, 256), BF16),
            pltpu.VMEM((2, 1024, 1024), BF16),
            pltpu.VMEM((2, 1024, 1024), BF16),
            pltpu.VMEM((2, 256, 256), BF16),
            pltpu.VMEM((ROWS * COLS, 128), F32),
            pltpu.VMEM((ROWS * COLS, 128), F32),
            dma,
            dma((STEPS,)), dma((STEPS,)),
            dma((STEPS, 2, 2)), dma((STEPS, 2, 2)),
            dma((STEPS, 2)), dma((STEPS, 2)),
            dma((STEPS, 2)), dma((STEPS, 2)),
        ],
        compiler_params=pltpu.CompilerParams(
            collective_id=0, has_side_effects=True, vmem_limit_bytes=67000000),
    )(distribution, density, cell_type, inflow.reshape(1, LOCAL))


def solution(mesh):
    placed = (P("gx", "gy", "vert"), P("gx", "gy"), P("gx", "gy"), P("vert"))
    return jax.shard_map(
        per_device, mesh=mesh, in_specs=placed, out_specs=P("gx", "gy", "vert"), check_vma=False
    )
```

time: 91.3 us -> 79.4 us (0.87)
  Pallas kernels: 88 us -> 76.1 us
    pallas_call x1, Pallas kernels: 88 us -> 76.1 us  [per_device(): pl.pallas_call(kernel, out_shape=jax.ShapeDtypeStruct((ROWS, COLS, LOCAL)...]
where the time goes in v1:
time: 79.4 us; the launch traced here: 79.2 us
  Pallas kernels  76.1 us (96%)
  local copies, waits for them, and re-layouts  3.14 us (4%)
    pallas_call x1, Pallas kernels, per_device(): pl.pallas_call(kernel, out_shape=jax.ShapeDtypeStruct((ROWS, COLS, LOCAL)...  76.1 us
    unnamed x1, local copies, waits for them, and re-layouts  3.14 us

profile of v1, /device:TPU:33, one launch (start us, length us, event | category | flops | bytes accessed | tf_op | source)
XLA Modules:
  0.0 79.2 jit_solution(3274629958103387684)
XLA Ops:
  0.0 76.1 %shard_map.46 = f32[16,16,2048]{2,1,0:T(8,128)} custom-call(f32[16,16,2048]{2,1,0:T(8,128)} %dist.1, f32[16,16]{1,0:T(8,128)} %density.1, s32[16,16]{1,0:T(8,128)} %cell_type.1, f32[1,2048]{1,0:T(1,128)} %bitcast.1), custom_call_target="tpu_custom_call" | custom-call | tf_op jit(solution)/shard_map/pallas_call | solution.py:397
  76.1 3.1 %copy.6 = f32[16,16,2048]{2,1,0:T(8,128)} copy(f32[16,16,2048]{2,1,0:T(8,128)} %shard_map.46) | data formatting | bytes 4194304

commit v2 on v1

--- a/solution.py
+++ b/solution.py
@@ -107,14 +107,14 @@
     lax.fori_loop(0, 256, tile, 0)
 
 
-def advect(vt, pad, base, adv):
+def advect(vt, pad, base, start, count, adv):
     lane = iota((1, 128), 1)
     vy = (as_f32(lane % 64) - 0.5 * (NVX - 1)) * SPACING
     ay = TIME_STEP * jnp.abs(vy)
     cy = 0.5 * ay * (1.0 - ay)
     forward = jnp.broadcast_to(vy > 0, (COLS, 128))
     sign = 2 * vt - 1
-    offset = (1 - vt) * (GROUP - 1)
+    offset = start + (1 - vt) * (count - 1)
     first = 2 + base + offset
 
     def chunk(m, carry):
@@ -130,7 +130,7 @@
         here = row(first)
         d0 = here - u1
         s1 = clamp_slope(u1 - u2, d0)
-        for k in range(GROUP):
+        for k in range(count):
             px = first + k * sign
             ahead = row(px + sign)
             dw = ahead - here
@@ -318,8 +318,14 @@
     def back(step, group):
         return partner_copy(gown, gin, qsend, qrecv, step, group)
 
-    def stage_a(step, group):
-        advect(vt, pads.at[step], bases[group], adv.at[group])
+    def stage_a(step, group, start=0, count=GROUP):
+        advect(vt, pads.at[step], bases[group], start, count, adv.at[group])
+
+    def stage_a_inner(step):
+        stage_a(step, 0, 2 * gx, GROUP - 2)
+
+    def stage_a_edge(step):
+        stage_a(step, 0, (1 - gx) * (GROUP - 2), 2)
 
     def stage_t(step, group):
         to_parities(vt, adv.at[group], h_ref, t_ref, yown.at[step, group])
@@ -358,31 +364,24 @@
     parity_maps(vt, h_ref)
     make_kernel_blocks(vt, khi, klo)
 
-    take_y(0, 1)
-    stage_a(0, 1)
-    take_y(0, 0)
-    take_x(0)
-    stage_a(0, 0)
-    stage_t(0, 0)
-    stage_t(0, 1)
-    stage_c(0, 0)
-    stage_c(0, 1)
-    stage_f(0, 0)
-    send_x(1)
-    send_y(1, 0)
-    stage_f(0, 1)
-    send_y(1, 1)
-    take_y(1, 1)
-    stage_a(1, 1)
-    stage_t(1, 1)
-    stage_c(1, 1)
-    take_y(1, 0)
-    take_x(1)
-    stage_a(1, 0)
-    stage_t(1, 0)
-    stage_f(1, 1)
-    stage_c(1, 0)
-    stage_f(1, 0)
+    for step in range(STEPS):
+        take_y(step, 1)
+        stage_a(step, 1)
+        stage_t(step, 1)
+        take_y(step, 0)
+        stage_a_inner(step)
+        stage_c(step, 1)
+        take_x(step)
+        stage_a_edge(step)
+        stage_t(step, 0)
+        stage_f(step, 1)
+        if step < STEPS - 1:
+            send_y(step + 1, 1)
+        stage_c(step, 0)
+        stage_f(step, 0)
+        if step < STEPS - 1:
+            send_x(step + 1)
+            send_y(step + 1, 0)
     for step in range(STEPS):
         wait_sent(step)
         for group in range(2):

time: 79.4 us -> 74.9 us (0.943)
  Pallas kernels: 76.1 us -> 71.6 us
    pallas_call x1, Pallas kernels: 76.1 us -> 71.6 us  [per_device(): pl.pallas_call(kernel, out_shape=jax.ShapeDtypeStruct((ROWS, COLS, LOCAL)...]
where the time goes in v2:
time: 74.9 us; the launch traced here: 74.7 us
  Pallas kernels  71.6 us (96%)
  local copies, waits for them, and re-layouts  3.14 us (4%)
    pallas_call x1, Pallas kernels, per_device(): pl.pallas_call(kernel, out_shape=jax.ShapeDtypeStruct((ROWS, COLS, LOCAL)...  71.6 us
    unnamed x1, local copies, waits for them, and re-layouts  3.14 us

profile of v2, /device:TPU:33, one launch (start us, length us, event | category | flops | bytes accessed | tf_op | source)
XLA Modules:
  0.0 74.7 jit_solution(461483703150707296)
XLA Ops:
  0.0 71.6 %shard_map.46 = f32[16,16,2048]{2,1,0:T(8,128)} custom-call(f32[16,16,2048]{2,1,0:T(8,128)} %dist.1, f32[16,16]{1,0:T(8,128)} %density.1, s32[16,16]{1,0:T(8,128)} %cell_type.1, f32[1,2048]{1,0:T(1,128)} %bitcast.1), custom_call_target="tpu_custom_call" | custom-call | tf_op jit(solution)/shard_map/pallas_call | solution.py:396
  71.6 3.1 %copy.6 = f32[16,16,2048]{2,1,0:T(8,128)} copy(f32[16,16,2048]{2,1,0:T(8,128)} %shard_map.46) | data formatting | bytes 4194304

commit v3 on v2

--- a/solution.py
+++ b/solution.py
@@ -158,54 +158,64 @@
     return pl.ds(pl.multiple_of(n * 256, 256), 256)
 
 
-def stack(n, value, t_ref):
+def stack(n, count, value, t_ref):
     hi, lo = split(value)
-    t_ref[128 * n:128 * n + 128, :] = hi
-    t_ref[1024 + 128 * n:1024 + 128 * n + 128, :] = lo
-
-
-def to_parities(vt, adv, h_ref, t_ref, y_ref):
-    cells = adv.reshape(CELLS, LOCAL)
+    t_ref[count * n:count * n + count, :] = hi
+    t_ref[count * (8 + n):count * (8 + n) + count, :] = lo
+
+
+def joined(n, count, value):
+    return value[count * n:count * n + count] + value[count * (8 + n):count * (8 + n) + count]
+
+
+def cell_range(row, rows):
+    return pl.ds(pl.multiple_of(row * COLS, 2 * COLS), rows * COLS)
+
+
+def to_parities(vt, adv, row, rows, h_ref, t_ref, y_ref):
+    cells, count, at = adv.reshape(CELLS, LOCAL), rows * COLS, cell_range(row, rows)
     for n in range(8):
-        stack(n, cells[:, wide(jnp.where(vt == 1, n, 7 - n))], t_ref)
-    y = mm(t_ref[...], h_ref[0])
+        stack(n, count, cells[at, wide(jnp.where(vt == 1, n, 7 - n))], t_ref)
+    y = mm(t_ref[:16 * count], h_ref[0])
     for n in range(8):
-        value = y[128 * n:128 * n + 128] + y[1024 + 128 * n:1024 + 128 * n + 128]
+        value = joined(n, count, y)
         for odd in range(2):
-            y_ref[odd, :, 128 * n:128 * n + 128] = value[:, 128 * odd:128 * odd + 128]
-
-
-def contract(vt, own, other, khi, klo, g_ref):
+            y_ref[odd, at, 128 * n:128 * n + 128] = value[:, 128 * odd:128 * odd + 128]
+
+
+def contract(vt, own, other, khi, klo, g_ref, send):
     sign = as_f32(1 - 2 * vt)
     for k in range(2):
         hi, lo = split(own[k] + sign * other[k])
         both = mm(jnp.concatenate([hi, lo], axis=0), khi[k])
         g_ref[k] = both[:CELLS] + both[CELLS:] + mm(hi, klo[k])
-
-
-def from_parities(vt, own, other, h_ref, t_ref, adv, dens, kinds, inflow, put):
+        send(k)
+
+
+def from_parities(vt, own, other, row, rows, h_ref, t_ref, adv, dens, kinds, inflow, put):
     sign = as_f32(2 * vt - 1)
-    cells = adv.reshape(CELLS, LOCAL)
+    cells, count, at = adv.reshape(CELLS, LOCAL), rows * COLS, cell_range(row, rows)
     for n in range(8):
-        at = slice(128 * n, 128 * n + 128)
-        stack(n, jnp.concatenate([own[k, :, at] + sign * other[k, :, at] for k in range(2)], axis=1), t_ref)
-    back = mm(t_ref[...], h_ref[1])
+        lanes = slice(128 * n, 128 * n + 128)
+        both = [own[k, at, lanes] + sign * other[k, at, lanes] for k in range(2)]
+        stack(n, count, jnp.concatenate(both, axis=1), t_ref)
+    back = mm(t_ref[:16 * count], h_ref[1])
     lane = iota((1, 256), 1)
     vy = (as_f32(lane % 64) - 0.5 * (NVX - 1)) * SPACING
-    rate, kind = (jnp.concatenate([ref[...]] * 2, axis=1) for ref in (dens, kinds))
+    rate, kind = (jnp.concatenate([ref[at, :]] * 2, axis=1) for ref in (dens, kinds))
     for n in range(8):
         m = jnp.where(vt == 1, n, 7 - n)
-        gain = (back[128 * n:128 * n + 128] + back[1024 + 128 * n:1024 + 128 * n + 128]) * GAIN_SCALE
+        gain = joined(n, count, back) * GAIN_SCALE
         vx = (as_f32(vt * HALF + m * 4 + lane // 64) - 0.5 * (NVX - 1)) * SPACING
         nu = 1.0 + (vx * vx + vy * vy) / 8.0
-        a = cells[:, wide(m)]
+        a = cells[at, wide(m)]
         after = a + rate * (gain - nu * a)
         after = jnp.where(kind == 1, 0.0, jnp.where(kind == 2, inflow[:, wide(m)], after))
-        put(wide(m), after.reshape(GROUP, COLS, 256))
-
-
-def kernel(dist, density, cell_type, inflow, out, pads, packs, halos, adv, yown, yin, gown, gin, t_ref,
-           khi, klo, h_ref, dens_b, type_b, load_sem, xsend, xrecv, ysend, yrecv, fsend, frecv, qsend, qrecv):
+        put(wide(m), after.reshape(rows, COLS, 256))
+
+
+def kernel(dist, density, cell_type, inflow, result, pads, packs, halos, adv, yown, yin, gown, gin, t_ref,
+           khi, klo, h_ref, dens_b, type_b, out, load_sem, store_sem, xsend, xrecv, ysend, yrecv, fsend, frecv, qsend, qrecv):
     gx, gy, vt = lax.axis_index("gx"), lax.axis_index("gy"), lax.axis_index("vert")
     last = lax.axis_size("gy") - 1
     has_left, has_right = gy > 0, gy < last
@@ -306,48 +316,61 @@
             for side, present in sides:
                 pl.when(present)(lambda side=side, group=group: y_copy(step, group, side, side).wait_send())
 
-    def partner_copy(src, dst, send, recv, step, group):
+    parts = ((0, 2 * gx, GROUP - 2), (0, (1 - gx) * (GROUP - 2), 2), (1, 0, GROUP))
+
+    def store(part):
+        group, row, rows = parts[part]
+        at = pl.ds(bases[group] + row, rows)
+        return pltpu.make_async_copy(out.at[at], result.at[at], store_sem.at[part])
+
+    def there(step, part):
+        group, row, rows = parts[part]
+        at = cell_range(row, rows)
         return pltpu.make_async_remote_copy(
-            src_ref=src.at[step, group], dst_ref=dst.at[step, group],
-            send_sem=send.at[step, group], recv_sem=recv.at[step, group],
+            src_ref=yown.at[step, group, :, at, :], dst_ref=yin.at[step, group, :, at, :],
+            send_sem=fsend.at[step, part], recv_sem=frecv.at[step, part],
             device_id=(gx, gy, 1 - vt), device_id_type=MESH)
 
-    def there(step, group):
-        return partner_copy(yown, yin, fsend, frecv, step, group)
-
-    def back(step, group):
-        return partner_copy(gown, gin, qsend, qrecv, step, group)
-
-    def stage_a(step, group, start=0, count=GROUP):
-        advect(vt, pads.at[step], bases[group], start, count, adv.at[group])
-
-    def stage_a_inner(step):
-        stage_a(step, 0, 2 * gx, GROUP - 2)
-
-    def stage_a_edge(step):
-        stage_a(step, 0, (1 - gx) * (GROUP - 2), 2)
-
-    def stage_t(step, group):
-        to_parities(vt, adv.at[group], h_ref, t_ref, yown.at[step, group])
-        there(step, group).start()
+    def back(step, group, k):
+        return pltpu.make_async_remote_copy(
+            src_ref=gown.at[step, group, k], dst_ref=gin.at[step, group, k],
+            send_sem=qsend.at[step, group, k], recv_sem=qrecv.at[step, group, k],
+            device_id=(gx, gy, 1 - vt), device_id_type=MESH)
+
+    def stage_a(step, part):
+        group, row, rows = parts[part]
+        advect(vt, pads.at[step], bases[group], row, rows, adv.at[group])
+
+    def stage_t(step, part):
+        group, row, rows = parts[part]
+        to_parities(vt, adv.at[group], row, rows, h_ref, t_ref, yown.at[step, group])
+        there(step, part).start()
 
     def stage_c(step, group):
-        there(step, group).wait_recv()
-        contract(vt, yown.at[step, group], yin.at[step, group], khi, klo, gown.at[step, group])
-        back(step, group).start()
-
-    def stage_f(step, group):
-        back(step, group).wait_recv()
+        for part in ((0, 1), (2,))[group]:
+            there(step, part).wait_recv()
+        contract(vt, yown.at[step, group], yin.at[step, group], khi, klo, gown.at[step, group],
+                 lambda k: back(step, group, k).start())
+
+    def stage_f(step, part):
+        group, row, rows = parts[part]
         base = bases[group]
         if step < STEPS - 1:
             def put(lanes, value):
-                pads[step + 1, pl.ds(2 + base, GROUP), TOP:TOP + COLS, lanes] = value
+                pads[step + 1, pl.ds(2 + base + row, rows), TOP:TOP + COLS, lanes] = value
         else:
             def put(lanes, value):
-                out[pl.ds(base, GROUP), :, lanes] = value
+                out[pl.ds(base + row, rows), :, lanes] = value
         cells = pl.ds(pl.multiple_of(base * COLS, CELLS), CELLS)
-        from_parities(vt, gown.at[step, group], gin.at[step, group], h_ref, t_ref, adv.at[group],
+        from_parities(vt, gown.at[step, group], gin.at[step, group], row, rows, h_ref, t_ref, adv.at[group],
                       dens_b.at[cells], type_b.at[cells], inflow, put)
+
+        if step == STEPS - 1:
+            store(part).start()
+
+    def take_gains(step, group):
+        for k in range(2):
+            back(step, group, k).wait_recv()
 
     load.wait()
     pl.semaphore_wait(barrier, 2 + has_left.astype(jnp.int32) + has_right.astype(jnp.int32))
@@ -365,28 +388,38 @@
     make_kernel_blocks(vt, khi, klo)
 
     for step in range(STEPS):
+        final = step == STEPS - 1
         take_y(step, 1)
+        stage_a(step, 2)
+        stage_t(step, 2)
+        take_y(step, 0)
+        stage_a(step, 0)
+        stage_t(step, 0)
+        stage_c(step, 1)
+        take_x(step)
         stage_a(step, 1)
         stage_t(step, 1)
-        take_y(step, 0)
-        stage_a_inner(step)
-        stage_c(step, 1)
-        take_x(step)
-        stage_a_edge(step)
-        stage_t(step, 0)
-        stage_f(step, 1)
-        if step < STEPS - 1:
+        take_gains(step, 1)
+        stage_f(step, 2)
+        if not final:
             send_y(step + 1, 1)
         stage_c(step, 0)
+        take_gains(step, 0)
+        stage_f(step, 1)
+        if not final:
+            send_x(step + 1)
         stage_f(step, 0)
-        if step < STEPS - 1:
-            send_x(step + 1)
+        if not final:
             send_y(step + 1, 0)
+    for part in range(3):
+        store(part).wait()
     for step in range(STEPS):
         wait_sent(step)
+        for part in range(3):
+            there(step, part).wait_send()
         for group in range(2):
-            there(step, group).wait_send()
-            back(step, group).wait_send()
+            for k in range(2):
+                back(step, group, k).wait_send()
 
 
 def per_device(distribution, density, cell_type, inflow):
@@ -397,7 +430,7 @@
         kernel,
         out_shape=jax.ShapeDtypeStruct((ROWS, COLS, LOCAL), F32),
         in_specs=[pl.BlockSpec(memory_space=pl.ANY), vmem, vmem, vmem],
-        out_specs=vmem,
+        out_specs=pl.BlockSpec(memory_space=pl.ANY),
         scratch_shapes=[
             pltpu.VMEM((STEPS, PAD_X, PAD_Y, LOCAL), F32),
             pltpu.VMEM((STEPS, 2, 2, 2, 8, LOCAL), F32),
@@ -410,14 +443,15 @@
             pltpu.VMEM((2, 256, 256), BF16),
             pltpu.VMEM((ROWS * COLS, 128), F32),
             pltpu.VMEM((ROWS * COLS, 128), F32),
-            dma,
+            pltpu.VMEM((ROWS, COLS, LOCAL), F32),
+            dma, dma((3,)),
             dma((STEPS,)), dma((STEPS,)),
             dma((STEPS, 2, 2)), dma((STEPS, 2, 2)),
-            dma((STEPS, 2)), dma((STEPS, 2)),
-            dma((STEPS, 2)), dma((STEPS, 2)),
+            dma((STEPS, 3)), dma((STEPS, 3)),
+            dma((STEPS, 2, 2)), dma((STEPS, 2, 2)),
         ],
         compiler_params=pltpu.CompilerParams(
-            collective_id=0, has_side_effects=True, vmem_limit_bytes=67000000),
+            collective_id=0, has_side_effects=True, vmem_limit_bytes=46 << 20),
     )(distribution, density, cell_type, inflow.reshape(1, LOCAL))
 
 

time: 74.9 us -> 73.4 us (0.980)
  Pallas kernels: 71.6 us -> 68.1 us
  local copies, waits for them, and re-layouts: 3.14 us -> 5 us
    pallas_call x1, Pallas kernels: 71.6 us -> 68.1 us  [per_device(): pl.pallas_call(kernel, out_shape=jax.ShapeDtypeStruct((ROWS, COLS, LOCAL)...]
    unnamed x1 -> x9, local copies, waits for them, and re-layouts: 3.14 us -> 5 us
where the time goes in v3:
time: 73.4 us; the launch traced here: 73.1 us
  Pallas kernels  68.1 us (93%)
  local copies, waits for them, and re-layouts  5 us (7%)
    pallas_call x1, Pallas kernels, per_device(): pl.pallas_call(kernel, out_shape=jax.ShapeDtypeStruct((ROWS, COLS, LOCAL)...  68.1 us
    unnamed x9, local copies, waits for them, and re-layouts  5 us

profile of v3, /device:TPU:33, one launch (start us, length us, event | category | flops | bytes accessed | tf_op | source)
XLA Modules:
  0.0 73.1 jit_solution(4379290733044782128)
XLA Ops:
  0.0 0.0 copy-start
  0.0 1.6 %copy-done = f32[16,16,2048]{2,1,0:T(8,128)S(1)} copy-done((f32[16,16,2048]{2,1,0:T(8,128)S(1)}, f32[16,16,2048]{2,1,0:T(8,128)}, u32[]{:S(2)}) %copy-start) | copy-done | bytes 2097176
  1.6 0.0 copy-start.1
  1.6 0.7 copy-done.1
  2.3 0.0 copy-start.2
  2.3 0.7 copy-done.2
  3.0 0.0 copy-start.3
  3.0 0.7 copy-done.3
  3.7 68.1 %shard_map.46 = f32[16,16,2048]{2,1,0:T(8,128)S(1)} custom-call(f32[16,16,2048]{2,1,0:T(8,128)S(1)} %copy-done, f32[16,16]{1,0:T(8,128)S(1)} %copy-done.1, s32[16,16]{1,0:T(8,128)S(1)} %copy-done.2, f32[1,2048]{1,0:T(1,128)S(1)} %bitcast.1), custom_call_target="tpu_custom_call" | custom-call | tf_op jit(solution)/shard_map/pallas_call | solution.py:429
  71.8 1.3 %copy.6 = f32[16,16,2048]{2,1,0:T(8,128)} copy(f32[16,16,2048]{2,1,0:T(8,128)S(1)} %shard_map.46) | data formatting | bytes 4194304
Async XLA Ops:
  0.0 1.6 %copy-start = (f32[16,16,2048]{2,1,0:T(8,128)S(1)}, f32[16,16,2048]{2,1,0:T(8,128)}, u32[]{:S(2)}) copy-start(f32[16,16,2048]{2,1,0:T(8,128)} %dist.1) | copy-start | bytes 6291460
  1.6 0.7 copy-start.1
  2.3 0.7 copy-start.2
  3.0 0.7 copy-start.3

commit v4 on v3

--- a/solution.py
+++ b/solution.py
@@ -214,8 +214,8 @@
         put(wide(m), after.reshape(rows, COLS, 256))
 
 
-def kernel(dist, density, cell_type, inflow, result, pads, packs, halos, adv, yown, yin, gown, gin, t_ref,
-           khi, klo, h_ref, dens_b, type_b, out, load_sem, store_sem, xsend, xrecv, ysend, yrecv, fsend, frecv, qsend, qrecv):
+def kernel(dist, density_in, cell_type_in, inflow_in, result, pads, packs, halos, adv, yown, yin, gown, gin, t_ref,
+           khi, klo, h_ref, dens_b, type_b, out, density, cell_type, inflow, load_sem, store_sem, xsend, xrecv, ysend, yrecv, fsend, frecv, qsend, qrecv):
     gx, gy, vt = lax.axis_index("gx"), lax.axis_index("gy"), lax.axis_index("vert")
     last = lax.axis_size("gy") - 1
     has_left, has_right = gy > 0, gy < last
@@ -223,8 +223,12 @@
     sides = ((0, has_left), (1, has_right))
     bases = ((1 - gx) * GROUP, gx * GROUP)
 
-    load = pltpu.make_async_copy(dist, pads.at[0, pl.ds(2, ROWS), pl.ds(TOP, COLS), :], load_sem)
+    load = pltpu.make_async_copy(dist, pads.at[0, pl.ds(2, ROWS), pl.ds(TOP, COLS), :], load_sem.at[0])
     load.start()
+    small = [pltpu.make_async_copy(src, dst, load_sem.at[1 + k]) for k, (src, dst) in enumerate(
+        ((density_in, density), (cell_type_in, cell_type), (inflow_in, inflow)))]
+    for copy in small:
+        copy.start()
 
     barrier = pltpu.get_barrier_semaphore()
     pl.semaphore_signal(barrier, inc=1, device_id=(1 - gx, gy, vt), device_id_type=MESH)
@@ -379,6 +383,8 @@
         send_y(0, group)
     for step in range(STEPS):
         clear_missing(step)
+    for copy in small:
+        copy.wait()
     rate = (COLLISION_RATE * density[...]).T
     kind = as_f32(cell_type[...]).T
     for x in range(ROWS):
@@ -423,13 +429,12 @@
 
 
 def per_device(distribution, density, cell_type, inflow):
-    vmem = pl.BlockSpec(memory_space=pltpu.VMEM)
     dma = pltpu.SemaphoreType.DMA
     pair = pltpu.VMEM((STEPS, 2, 2, CELLS, 1024), F32)
     return pl.pallas_call(
         kernel,
         out_shape=jax.ShapeDtypeStruct((ROWS, COLS, LOCAL), F32),
-        in_specs=[pl.BlockSpec(memory_space=pl.ANY), vmem, vmem, vmem],
+        in_specs=[pl.BlockSpec(memory_space=pltpu.HBM)] * 4,
         out_specs=pl.BlockSpec(memory_space=pl.ANY),
         scratch_shapes=[
             pltpu.VMEM((STEPS, PAD_X, PAD_Y, LOCAL), F32),
@@ -444,7 +449,10 @@
             pltpu.VMEM((ROWS * COLS, 128), F32),
             pltpu.VMEM((ROWS * COLS, 128), F32),
             pltpu.VMEM((ROWS, COLS, LOCAL), F32),
-            dma, dma((3,)),
+            pltpu.VMEM((ROWS, COLS), F32),
+            pltpu.VMEM((ROWS, COLS), jnp.int32),
+            pltpu.VMEM((1, LOCAL), F32),
+            dma((4,)), dma((3,)),
             dma((STEPS,)), dma((STEPS,)),
             dma((STEPS, 2, 2)), dma((STEPS, 2, 2)),
             dma((STEPS, 3)), dma((STEPS, 3)),
@@ -452,7 +460,8 @@
         ],
         compiler_params=pltpu.CompilerParams(
             collective_id=0, has_side_effects=True, vmem_limit_bytes=46 << 20),
-    )(distribution, density, cell_type, inflow.reshape(1, LOCAL))
+    )(*(pltpu.with_memory_space_constraint(x, pltpu.HBM)
+        for x in (distribution, density, cell_type, inflow.reshape(1, LOCAL))))
 
 
 def solution(mesh):

time: 73.4 us -> 69.2 us (0.943)
  local copies, waits for them, and re-layouts: 5 us -> 1.32 us
    unnamed x9 -> x1, local copies, waits for them, and re-layouts: 5 us -> 1.32 us
where the time goes in v4:
time: 69.2 us; the launch traced here: 69.1 us
  Pallas kernels  67.8 us (98%)
  local copies, waits for them, and re-layouts  1.32 us (2%)
    pallas_call x1, Pallas kernels, per_device(): pl.pallas_call(kernel, out_shape=jax.ShapeDtypeStruct((ROWS, COLS, LOCAL)...  67.8 us

profile of v4, /device:TPU:33, one launch (start us, length us, event | category | flops | bytes accessed | tf_op | source)
XLA Modules:
  0.0 69.1 jit_solution(13748817243894714948)
XLA Ops:
  0.0 67.8 %shard_map.46 = f32[16,16,2048]{2,1,0:T(8,128)S(1)} custom-call(f32[16,16,2048]{2,1,0:T(8,128)} %dist.1, f32[16,16]{1,0:T(8,128)} %density_in.1, s32[16,16]{1,0:T(8,128)} %cell_type_in.1, f32[1,2048]{1,0:T(1,128)} %bitcast.1), custom_call_target="tpu_custom_call" | custom-call | tf_op jit(solution)/shard_map/pallas_call | solution.py:434
  67.8 1.3 %copy.6 = f32[16,16,2048]{2,1,0:T(8,128)} copy(f32[16,16,2048]{2,1,0:T(8,128)S(1)} %shard_map.46) | data formatting | bytes 4194304
